TPU v7x, 256 devices: a whole 4x4x8 slice. The times are simulated.
256 devices in a mesh: elem: 16 (over y_lo, z), pts: 16 (over y_hi, x, core).
Axes of the slice: x: 4, y: 4 (y_hi: 2, y_lo: 2; y = y_hi * 2 + y_lo), z: 8, core: 2. Of those that a mesh axis runs over, the one named last changes fastest.
Arguments:
- basis: float32 [64, 8192, 256], P('elem', 'pts'), may hold values from -6 to 6
- applied: float32 [64, 8192, 256], P('elem', 'pts'), may hold values from -6 to 6
- quad: float32 [64, 8192], P('elem', 'pts'), may hold values from 0.00017263349 to 0.00069053395
- face_index: int32 [64, 4, 1024], P('elem', None, 'pts'), may hold values from 0 to 511
- face_pairing: int32 [64, 1024], P('elem', 'pts'), may hold values from 0 to 63, as said below
- orbitals: float32 [16384, 2048], P('elem', 'pts'), may hold values from -6 to 6
Outputs:
- filtered: float32 [16384, 2048], P('elem', 'pts')
Inputs may be any that keep to these rules, and one draw needn't show every extreme that they name: `face_pairing`: each aligned block of 64 entries of a row is a permutation of 0 to 63.
All inputs are finite; a program needn't handle non-finite values.
Results may differ from a plain program's by a relative error of at most 0.0003.
Values sent between devices are 32-bit elements; how exact they have to be, the bound alone decides.
A program may use at most 64 MiB of HBM per device.

v0:
```python
import jax
import jax.numpy as jnp
from jax import lax
from jax.experimental import pallas as pl
from jax.experimental.pallas import tpu as pltpu
from jax.sharding import PartitionSpec as P

NB = 256
MESH = pl.DeviceIdType.MESH
F32 = jnp.float32
BF16 = jnp.bfloat16


def split(value):
    high = value.astype(BF16)
    low = (value - high.astype(F32)).astype(BF16)
    return high, low


def nn(left, right):
    return lax.dot_general(left, right, (((1,), (0,)), ((), ())), preferred_element_type=F32)


def nt(left, right):
    return lax.dot_general(left, right, (((1,), (1,)), ((), ())), preferred_element_type=F32)


def three(product, left, right):
    return product(left[0], right[0]) + (product(left[0], right[1]) + product(left[1], right[0]))


class Slots:
    def __init__(self):
        self.count = 0

    def take(self, number=1):
        first = self.count
        self.count += number
        return first


def layout():
    slots = Slots()
    table = {}
    for name, number in (
        ("lead", 1), ("vin", 1), ("vout", 1), ("pair", 3),
        ("relay", 6), ("raw", 6), ("final", 6), ("ysum", 3),
        ("gy", 2), ("gx", 8), ("gf", 4),
        ("vx", 4), ("vf", 2), ("vy", 4),
        ("up", 8), ("down", 8),
    ):
        table[name] = slots.take(number)
    return table, slots.count


TABLE, COPIES = layout()


def kernel(
    basis, applied, quad_in, index_in, pairing_in, orbitals, out,
    b_buf, a_buf, quad, face_index, face_pairing, bq, ta, tb, tl, vpart, cpart, vpair, cpair, vring, cring, y_in, yc_in, vblock, cblock,
    near_part, up_part, down_part, field, near_sum, up_out, up_in, down_in,
    local, send, recv,
):
    elem = lax.axis_index("elem")
    pts = lax.axis_index("pts")
    core = lax.rem(pts, 2)
    x = lax.rem(pts // 2, 4)
    yh = pts // 8
    other = 1 - core

    def at(elem_to, yh_to, x_to, core_to):
        return {"elem": lax.rem(elem_to, 16), "pts": yh_to * 8 + lax.rem(x_to, 4) * 2 + core_to}

    partner = at(elem, yh, x, other)
    xm = at(elem, yh, x + 3, core)
    xp = at(elem, yh, x + 1, core)
    yp = at(elem, 1 - yh, x, core)
    after = at(elem + core, yh, x, other)
    before = at(elem + 15 + core, yh, x, other)
    far = at(elem + 15 + 2 * core, yh, x, other)
    em = at(elem + 15, yh, x, core)
    ep = at(elem + 1, yh, x, core)

    started = []

    def remote(name, offset, source, target, device):
        index = TABLE[name] + offset
        return pltpu.make_async_remote_copy(
            src_ref=source, dst_ref=target, send_sem=send.at[index], recv_sem=recv.at[index],
            device_id=device, device_id_type=MESH,
        )

    def push(name, offset, source, target, device):
        copy = remote(name, offset, source, target, device)
        copy.start()
        started.append(copy)

    def arrive(name, offset, target):
        remote(name, offset, target, target, partner).wait_recv()

    def sent(name, offset, source):
        remote(name, offset, source, source, partner).wait_send()

    small = [
        pltpu.make_async_copy(index_in, face_index, local.at[9]),
        pltpu.make_async_copy(quad_in, quad, local.at[10]),
        pltpu.make_async_copy(pairing_in, face_pairing, local.at[11]),
    ]
    for copy in small:
        copy.start()
    for e in range(4):
        pltpu.make_async_copy(basis.at[e], b_buf.at[e], local.at[e]).start()
    own_rows = pl.ds(pl.multiple_of(core * 512, 512), 512)
    other_rows = pl.ds(pl.multiple_of(other * 512, 512), 512)
    for i in range(4):
        e = lax.rem(i + 2 * other, 4)
        pltpu.make_async_copy(applied.at[e], a_buf.at[e], local.at[4 + e]).start()
    own_field = pltpu.make_async_copy(orbitals.at[own_rows], field.at[0, core], local.at[8])
    own_field.start()

    barrier = pltpu.get_barrier_semaphore()
    for device in (partner, xm, xp, yp, far, em, ep):
        pl.semaphore_signal(barrier, inc=1, device_id=device, device_id_type=MESH)

    point = lax.broadcasted_iota(jnp.int32, (512, NB), 0)
    lane = lax.broadcasted_iota(jnp.int32, (NB, 128), 1)

    def traces(e, carry):
        pltpu.make_async_copy(basis.at[e], b_buf.at[e], local.at[e]).wait()

        @pl.when(e == 0)
        def _():
            for copy in small:
                copy.wait()

        turned = b_buf[e].T
        high, low = split(turned)
        picks = jnp.concatenate([face_index[e, r : r + 1, :] for r in (0, 2, 1, 3)], axis=1)
        chosen = jnp.where(point == picks, 1.0, 0.0).astype(BF16)
        values = nn(high, chosen) + nn(low, chosen)
        faces, inside = values[:, :128], values[:, 128:]
        ta[e] = faces
        tb[e] = inside
        tl[e] = jnp.where(lane < 64, faces, pltpu.roll(inside, 64, 1))
        high, low = split(turned * quad[pl.ds(e, 1), :])
        bq[0, e] = high
        bq[1, e] = low
        return carry

    def rows(first, size):
        return pl.ds(pl.multiple_of(first, 8), size)

    def volumes(i, carry):
        e = lax.rem(i + 2 * other, 4)
        half = i // 2
        first = lax.rem(i, 2) * 192
        pltpu.make_async_copy(applied.at[e], a_buf.at[e], local.at[4 + e]).wait()
        faces = ta[e]
        total = three(nn, (bq[0, e], bq[1, e]), split(a_buf[e]))
        total = total + three(nt, split((2.0 * faces + tb[e]) * (1.0 / 1024.0)), split(faces))
        vpart[half, rows(first, 128), :128] = total[:128, :128]
        vpart[half, rows(first, 128), 128:] = total[:128, 128:] + total[128:, :128].T
        vpart[half, rows(first + 128, 64), :128] = total[128:192, 128:]
        vpart[half, rows(first + 128, 64), 128:] = total[192:, 128:]

        @pl.when((i == 1) & (depth > 0))
        def _():
            remote("pair", 0, vpart.at[0], vpair, partner).start()

        return carry

    row = lax.broadcasted_iota(jnp.int32, (128, NB), 0)
    column = lax.broadcasted_iota(jnp.int32, (128, NB), 1)
    factor = jnp.where(
        column < 128,
        jnp.where(column < 64, 0.0, jnp.where(row < 64, -3.0, 0.5)),
        jnp.where(column < 192, 0.0, jnp.where(row < 64, -0.5, 0.0)),
    ) * (1.0 / 1024.0)
    slot = jnp.where(row < 64, row, row - 64)

    def couplings(i, carry):
        e = jnp.where((core == 1) | (i == 3), i, lax.rem(i + 2, 3))
        half = jnp.where(e // 2 == core, 1, 0)
        k = lax.rem(e, 2)

        @pl.when(i == 3)
        def _():
            arrive("lead", 0, tl.at[4])

        order = face_pairing[pl.ds(e, 1), :]
        order = jnp.concatenate([order] * 4, axis=1)
        mixing = jnp.where(slot == order, factor, 0.0).astype(BF16)
        high, low = split(jnp.concatenate([ta[e], tb[e]], axis=1))
        sides = nt(high, mixing) + nt(low, mixing)
        mine = rows(k * NB, NB)
        cpart[half, mine, :] = three(nt, split(sides), split(tl[e + 1]))

        @pl.when(half == 0)
        def _():
            remote("pair", 1 + k, cpart.at[0, mine], cpair.at[mine], partner).start()

        return carry

    def near(t):
        return lax.rem(t, 4)

    sizes = (32, 32, 24)

    def chunk(unit, t, s):
        if unit == 2:
            return rows(yh * 192 + near(t) * 48 + s * 24, 24)
        return rows(unit * NB + (near(t) * 2 + s) * 32, 32)

    def strip(t, half):
        return rows(half * 192 + near(t) * 48, 48)

    def part(unit):
        return vpart.at[1] if unit == 2 else cpart.at[1]

    def ring(unit, k):
        return vring.at[k] if unit == 2 else cring.at[unit, k]

    def ring_first(unit):
        acc = part(unit)
        push("relay", unit * 2, acc.at[chunk(unit, x + 2, 0)], ring(unit, 0), xm)
        push("relay", unit * 2 + 1, acc.at[chunk(unit, x + 2, 1)], ring(unit, 1), xp)
        push("raw", unit * 2 + 1, acc.at[chunk(unit, x + 3, 1)], ring(unit, 3), xm)
        push("raw", unit * 2, acc.at[chunk(unit, x + 1, 0)], ring(unit, 2), xp)

    def ring_second(unit):
        for s, shift, device in ((0, 3, xm), (1, 1, xp)):
            passing = ring(unit, s)
            arrive("relay", unit * 2 + s, passing)
            passing[...] = passing[...] + part(unit)[chunk(unit, x + shift, s), :]
            push("final", unit * 2 + s, passing, ring(unit, 4 + s), device)

    def ring_last(unit, target):
        for s in range(2):
            arrive("raw", unit * 2 + s, ring(unit, 2 + s))
            arrive("final", unit * 2 + s, ring(unit, 4 + s))
            where = chunk(unit, x, s)
            target[where, :] = part(unit)[where, :] + ring(unit, 2 + s)[...] + ring(unit, 4 + s)[...]

    def share(name, offset, block, where, device):
        push(name, offset, block.at[where], block.at[where], device)

    def couple_first(unit):
        where = rows(unit * NB, NB)
        arrive("pair", 1 + unit, cpair.at[where])
        cpart[1, where, :] = cpart[1, where, :] + cpair[where, :]
        ring_first(unit)

    def couple_third(unit):
        ring_last(unit, cpart.at[1])
        push("ysum", unit, cpart.at[1, chunk(unit, x, 1 - yh)], yc_in.at[unit], yp)

    def couple_fourth(unit):
        arrive("ysum", unit, yc_in.at[unit])
        where = chunk(unit, x, yh)
        cblock[where, :] = cpart[1, where, :] + yc_in[unit]
        share("gy", unit, cblock, where, yp)
        share("gx", unit * 4 + yh, cblock, where, xm)
        share("gx", unit * 4 + 2 + yh, cblock, where, xp)

    def couple_fifth(unit):
        where = chunk(unit, x, 1 - yh)
        arrive("gy", unit, cblock.at[where])
        share("gx", unit * 4 + 1 - yh, cblock, where, xm)
        share("gx", unit * 4 + 3 - yh, cblock, where, xp)

    def couple_forward(unit, s):
        where = chunk(unit, x + 1 + 2 * s, s)
        arrive("gx", unit * 4 + 3 * s, cblock.at[where])
        share("gf", unit * 2 + s, cblock, where, at(elem, yh, x + 3 - 2 * s, core))

    def couple_end(unit):
        arrive("gx", unit * 4 + 1, cblock.at[chunk(unit, x + 1, 1)])
        arrive("gx", unit * 4 + 2, cblock.at[chunk(unit, x + 3, 0)])
        for s in range(2):
            arrive("gf", unit * 2 + s, cblock.at[chunk(unit, x + 2, s)])

    def meet():
        pl.semaphore_wait(barrier, 7)
        remote("lead", 0, tl.at[0], tl.at[4], em).start()

    depth = lax.rem(elem, 8)
    lax.fori_loop(0, 4, traces, 0)
    pl.when(depth > 0)(meet)
    lax.fori_loop(0, 4, volumes, 0)
    @pl.when(depth == 0)
    def _():
        meet()
        remote("pair", 0, vpart.at[0], vpair, partner).start()

    arrive("pair", 0, vpair)
    vpart[1] = vpart[1] + vpair[...]
    push("ysum", 2, vpart.at[1, rows((1 - yh) * 192, 192)], y_in, yp)
    push("vin", 0, orbitals.at[other_rows], field.at[0, core], partner)
    lax.fori_loop(0, 4, couplings, 0)
    couple_first(0)
    couple_first(1)
    ring_second(0)
    ring_second(1)
    arrive("ysum", 2, y_in)
    mine = rows(yh * 192, 192)
    vpart[1, mine, :] = vpart[1, mine, :] + y_in[...]
    ring_first(2)
    couple_third(0)
    couple_third(1)
    ring_second(2)
    couple_fourth(0)
    ring_last(2, vblock)
    for s in range(2):
        share("vx", s, vblock, chunk(2, x, s), xm)
        share("vx", 2 + s, vblock, chunk(2, x, s), xp)
    share("vy", 0, vblock, strip(x, yh), yp)
    couple_fourth(1)
    couple_forward(0, yh)
    for s in range(2):
        where = chunk(2, x + 1 + 2 * s, s)
        arrive("vx", 3 * s, vblock.at[where])
        share("vf", s, vblock, where, (xm, xp)[s])
    arrive("vx", 1, vblock.at[chunk(2, x + 1, 1)])
    arrive("vx", 2, vblock.at[chunk(2, x + 3, 0)])
    share("vy", 1, vblock, strip(x + 1, yh), yp)
    share("vy", 2, vblock, strip(x + 3, yh), yp)
    couple_fifth(0)
    couple_forward(1, yh)
    couple_fifth(1)
    for s in range(2):
        arrive("vf", s, vblock.at[chunk(2, x + 2, s)])
    share("vy", 3, vblock, strip(x + 2, yh), yp)
    couple_forward(0, 1 - yh)
    couple_forward(1, 1 - yh)

    for number, shift in ((0, 0), (1, 1), (2, 3), (3, 2)):
        arrive("vy", number, vblock.at[strip(x + shift, 1 - yh)])
    diagonal = jnp.where(
        lax.broadcasted_iota(jnp.int32, (128, 128), 0) == lax.broadcasted_iota(jnp.int32, (128, 128), 1), 4.0 / 12.0, 0.0
    )
    def halved(block):
        return (block + block.T) * (0.5 / 12.0) - diagonal

    def near_store(first, second, block):
        high, low = split(block)
        near_part[0, first : first + block.shape[0], second : second + block.shape[1]] = high
        near_part[1, first : first + block.shape[0], second : second + block.shape[1]] = low

    for k in range(2):
        first = k * 192
        corner = k * NB
        near_store(corner, corner, halved(vblock[first : first + 128, :128]))
        cross = vblock[first : first + 128, 128:] * (0.5 / 12.0)
        near_store(corner, corner + 128, cross)
        near_store(corner + 128, corner, cross.T)
        last = jnp.concatenate([vblock[first + 128 : first + 192, :128], vblock[first + 128 : first + 192, 128:]], axis=0)
        near_store(corner + 128, corner + 128, halved(last))
    couple_end(0)
    couple_end(1)
    block = cblock[NB:, :] * (1.0 / 12.0)
    high, low = split(block)
    down_part[0] = high
    down_part[1] = low
    high, low = split(block.T)
    up_part[0] = high
    up_part[1] = low
    block = cblock[:NB, :] * (1.0 / 12.0)
    near_store(0, NB, block)
    near_store(NB, 0, block.T)
    own_field.wait()
    arrive("vin", 0, field.at[0, other])

    def doubled(value):
        high, low = split(value)
        return jnp.concatenate([high, low], axis=1)

    def times(matrix, pair):
        both = nn(matrix[0], pair)
        return both[:, :128] + (both[:, 128:] + nn(matrix[1], pair[:, :128]))

    def halo(name, n, j):
        if name == "up":
            return remote("up", n * 2 + j, up_out.at[n, j], up_in.at[n, j], after)
        return remote("down", n * 2 + j, field.at[n, j, pl.ds(0, 256)], down_in.at[n, j], before)

    def filter_step(m, carry):
        n = jnp.maximum(m - 1, 0)
        oldest = jnp.maximum(m - 2, 0)
        scale = jnp.where(m == 1, 1.0, 2.0)
        keep = jnp.where(m == 1, 0.0, 1.0)

        @pl.when(m > 0)
        def _():
            parts = [split(field[n, j]) for j in range(2)]
            high = jnp.concatenate([parts[0][0], parts[1][0]], axis=1)
            low = jnp.concatenate([parts[0][1], parts[1][1]], axis=1)
            near_sum[...] = nn(near_part[0], high) + (nn(near_part[0], low) + nn(near_part[1], high))

        def column_step(j, inner):
            lanes = pl.ds(pl.multiple_of(j * 128, 128), 128)

            @pl.when(m > 0)
            def _():
                halo("up", n, j).wait_recv()
                value = scale * (near_sum[:256, lanes] + up_in[n, j])
                field[m, j, :256, :] = value - keep * field[oldest, j, :256, :]

            @pl.when(m < 4)
            def _():
                halo("down", m, j).start()

            @pl.when(m > 0)
            def _():
                halo("down", n, j).wait_recv()
                value = scale * (near_sum[256:, lanes] + times(down_part, doubled(down_in[n, j])))
                field[m, j, 256:, :] = value - keep * field[oldest, j, 256:, :]

            @pl.when(m < 4)
            def _():
                up_out[m, j] = times(up_part, doubled(field[m, j, 256:, :]))
                halo("up", m, j).start()

            @pl.when((m == 4) & (j == other))
            def _():
                remote("vout", 0, field.at[4, other], out.at[own_rows], partner).start()

            return inner

        return lax.fori_loop(0, 2, column_step, carry)

    lax.fori_loop(0, 5, filter_step, 0)
    out[own_rows, :] = field[4, core]

    def drain(k, carry):
        n, j = k // 2, lax.rem(k, 2)
        halo("up", n, j).wait_send()
        halo("down", n, j).wait_send()
        return carry

    lax.fori_loop(0, 8, drain, 0)
    for copy in started:
        copy.wait_send()
    sent("lead", 0, tl.at[0])
    sent("pair", 0, vpart.at[0])
    for unit in range(2):
        sent("pair", 1 + unit, cpart.at[0, rows(unit * NB, NB)])
    sent("vout", 0, field.at[4, other])
    arrive("vout", 0, out.at[other_rows])


def body(basis, applied, quad, face_index, face_pairing, orbitals):
    anywhere = pl.BlockSpec(memory_space=pl.ANY)
    return pl.pallas_call(
        kernel,
        out_shape=pltpu.VMEM(orbitals.shape, F32),
        in_specs=[anywhere] * 6,
        out_specs=pl.BlockSpec(memory_space=pltpu.VMEM),
        scratch_shapes=[
            pltpu.VMEM((4, 512, NB), F32),
            pltpu.VMEM((4, 512, NB), F32),
            pltpu.VMEM(quad.shape, F32),
            pltpu.VMEM(face_index.shape, jnp.int32),
            pltpu.VMEM(face_pairing.shape, jnp.int32),
            pltpu.VMEM((2, 4, NB, 512), BF16),
            pltpu.VMEM((4, NB, 128), F32),
            pltpu.VMEM((4, NB, 128), F32),
            pltpu.VMEM((5, NB, 128), F32),
            pltpu.VMEM((2, 384, NB), F32),
            pltpu.VMEM((2, 512, NB), F32),
            pltpu.VMEM((384, NB), F32),
            pltpu.VMEM((512, NB), F32),
            pltpu.VMEM((6, 24, NB), F32),
            pltpu.VMEM((2, 6, 32, NB), F32),
            pltpu.VMEM((192, NB), F32),
            pltpu.VMEM((2, 32, NB), F32),
            pltpu.VMEM((384, NB), F32),
            pltpu.VMEM((512, NB), F32),
            pltpu.VMEM((2, 512, 512), BF16),
            pltpu.VMEM((2, NB, NB), BF16),
            pltpu.VMEM((2, NB, NB), BF16),
            pltpu.VMEM((5, 2, 512, 128), F32),
            pltpu.VMEM((512, NB), F32),
            pltpu.VMEM((4, 2, NB, 128), F32),
            pltpu.VMEM((4, 2, NB, 128), F32),
            pltpu.VMEM((4, 2, NB, 128), F32),
            pltpu.SemaphoreType.DMA((12,)),
            pltpu.SemaphoreType.DMA((COPIES,)),
            pltpu.SemaphoreType.DMA((COPIES,)),
        ],
        name="filtered",
        compiler_params=pltpu.CompilerParams(collective_id=0, has_side_effects=True),
    )(basis, applied, quad, face_index, face_pairing, orbitals)


def solution(mesh):
    return jax.shard_map(
        body,
        mesh=mesh,
        in_specs=(
            P("elem", "pts", None),
            P("elem", "pts", None),
            P("elem", "pts"),
            P("elem", None, "pts"),
            P("elem", "pts"),
            P("elem", "pts"),
        ),
        out_specs=P("elem", "pts"),
        check_vma=False,
    )
```

profile of v0, /device:TPU:1, one launch (start us, length us, event | category | flops | bytes accessed | tf_op | source)
XLA Modules:
  0.0 61.6 jit_solution(5332743461440504799)
XLA Ops:
  0.0 60.8 %filtered.1 = f32[1024,128]{1,0:T(8,128)S(1)} custom-call(f32[4,512,256]{2,1,0:T(8,128)} %basis.1, f32[4,512,256]{2,1,0:T(8,128)} %applied.1, f32[4,512]{1,0:T(4,128)} %quad_in.1, s32[4,4,64]{2,1,0:T(4,128)} %index_in.1, s32[4,64]{1,0:T(4,128)} %pairing_in.1, f32[1024,128]{1,0:T(8,128)} %orbitals.1), custom_call_target="tpu_custom_call" | custom-call | tf_op jit(solution)/shard_map/filtered/pallas_call | solution.py:454
  60.9 0.8 %copy.8 = f32[1024,128]{1,0:T(8,128)} copy(f32[1024,128]{1,0:T(8,128)S(1)} %filtered.1) | data formatting | bytes 1048576
where the time goes:
time: 61.7 us; the launch traced here: 61.6 us
  Pallas kernels  60.8 us (99%)
  local copies, waits for them, and re-layouts  0.8 us (1%)
    pallas_call x1, Pallas kernels, body(): pl.pallas_call(kernel, out_shape=pltpu.VMEM(orbitals.shape, F32), in_spec...  60.8 us

commit v1 on v0

v1 whole, which is shorter than its diff:
```python
import jax
import jax.numpy as jnp
from jax import lax
from jax.experimental import pallas as pl
from jax.experimental.pallas import tpu as pltpu
from jax.sharding import PartitionSpec as P

NB = 256
MESH = pl.DeviceIdType.MESH
NEAR = ((2, 1), (1, 1), (3, 1), (2, 0), (0, 1), (1, 0), (3, 0))
F32 = jnp.float32
BF16 = jnp.bfloat16


def split(value):
    high = value.astype(BF16)
    low = (value - high.astype(F32)).astype(BF16)
    return high, low


def nn(left, right):
    return lax.dot_general(left, right, (((1,), (0,)), ((), ())), preferred_element_type=F32)


def nt(left, right):
    return lax.dot_general(left, right, (((1,), (1,)), ((), ())), preferred_element_type=F32)


def three(product, left, right):
    return product(left[0], right[0]) + (product(left[0], right[1]) + product(left[1], right[0]))


class Slots:
    def __init__(self):
        self.count = 0

    def take(self, number=1):
        first = self.count
        self.count += number
        return first


def layout():
    slots = Slots()
    table = {}
    for name, number in (
        ("lead", 1), ("vin", 1), ("vout", 1), ("pair", 3), ("scatter", 21), ("gather", 21), ("up", 8), ("down", 8),
    ):
        table[name] = slots.take(number)
    return table, slots.count


TABLE, COPIES = layout()


def kernel(
    basis, applied, quad_in, index_in, pairing_in, orbitals, out,
    b_buf, a_buf, quad, face_index, face_pairing, bq, ta, tb, tl, vpart, cpart, vpair, cpair, v_in, c_in, vblock, cblock,
    near_part, up_part, down_part, field, near_sum, up_out, up_in, down_in,
    local, send, recv,
):
    elem = lax.axis_index("elem")
    pts = lax.axis_index("pts")
    core = lax.rem(pts, 2)
    x = lax.rem(pts // 2, 4)
    yh = pts // 8
    other = 1 - core

    def at(elem_to, yh_to, x_to, core_to):
        return {"elem": lax.rem(elem_to, 16), "pts": yh_to * 8 + lax.rem(x_to, 4) * 2 + core_to}

    partner = at(elem, yh, x, other)
    chips = [(lax.rem(x + dx, 4), yh if dy == 0 else 1 - yh) for dx, dy in NEAR]
    peers = [at(elem, half, t, core) for t, half in chips]
    after = at(elem + core, yh, x, other)
    before = at(elem + 15 + core, yh, x, other)
    far = at(elem + 15 + 2 * core, yh, x, other)
    em = at(elem + 15, yh, x, core)
    ep = at(elem + 1, yh, x, core)

    started = []

    def remote(name, offset, source, target, device):
        index = TABLE[name] + offset
        return pltpu.make_async_remote_copy(
            src_ref=source, dst_ref=target, send_sem=send.at[index], recv_sem=recv.at[index],
            device_id=device, device_id_type=MESH,
        )

    def push(name, offset, source, target, device):
        copy = remote(name, offset, source, target, device)
        copy.start()
        started.append(copy)

    def arrive(name, offset, target):
        remote(name, offset, target, target, partner).wait_recv()

    def sent(name, offset, source):
        remote(name, offset, source, source, partner).wait_send()

    small = [
        pltpu.make_async_copy(index_in, face_index, local.at[9]),
        pltpu.make_async_copy(quad_in, quad, local.at[10]),
        pltpu.make_async_copy(pairing_in, face_pairing, local.at[11]),
    ]
    for copy in small:
        copy.start()
    for e in range(4):
        pltpu.make_async_copy(basis.at[e], b_buf.at[e], local.at[e]).start()
    own_rows = pl.ds(pl.multiple_of(core * 512, 512), 512)
    other_rows = pl.ds(pl.multiple_of(other * 512, 512), 512)
    own_field = pltpu.make_async_copy(orbitals.at[own_rows], field.at[0, core], local.at[8])

    barrier = pltpu.get_barrier_semaphore()
    for device in [partner, far, em, ep] + peers:
        pl.semaphore_signal(barrier, inc=1, device_id=device, device_id_type=MESH)

    point = lax.broadcasted_iota(jnp.int32, (512, NB), 0)
    lane = lax.broadcasted_iota(jnp.int32, (NB, 128), 1)

    def traces(e, carry):
        pltpu.make_async_copy(basis.at[e], b_buf.at[e], local.at[e]).wait()

        @pl.when(e == 0)
        def _():
            for copy in small:
                copy.wait()

        later = lax.rem(e + 2 * other, 4)
        pltpu.make_async_copy(applied.at[later], a_buf.at[later], local.at[4 + later]).start()
        turned = b_buf[e].T
        high, low = split(turned)
        picks = jnp.concatenate([face_index[e, r : r + 1, :] for r in (0, 2, 1, 3)], axis=1)
        chosen = jnp.where(point == picks, 1.0, 0.0).astype(BF16)
        values = nn(high, chosen) + nn(low, chosen)
        faces, inside = values[:, :128], values[:, 128:]
        ta[e] = faces
        tb[e] = inside
        tl[e] = jnp.where(lane < 64, faces, pltpu.roll(inside, 64, 1))
        high, low = split(turned * quad[pl.ds(e, 1), :])
        bq[0, e] = high
        bq[1, e] = low
        return carry

    def rows(first, size):
        return pl.ds(pl.multiple_of(first, 8), size)

    def volumes(i, carry):
        e = lax.rem(i + 2 * other, 4)
        half = i // 2
        first = lax.rem(i, 2) * 192
        pltpu.make_async_copy(applied.at[e], a_buf.at[e], local.at[4 + e]).wait()
        faces = ta[e]
        total = three(nn, (bq[0, e], bq[1, e]), split(a_buf[e]))
        total = total + three(nt, split((2.0 * faces + tb[e]) * (1.0 / 1024.0)), split(faces))
        vpart[half, rows(first, 128), :128] = total[:128, :128]
        vpart[half, rows(first, 128), 128:] = total[:128, 128:] + total[128:, :128].T
        vpart[half, rows(first + 128, 64), :128] = total[128:192, 128:]
        vpart[half, rows(first + 128, 64), 128:] = total[192:, 128:]

        @pl.when((i == 1) & (depth > 0))
        def _():
            remote("pair", 0, vpart.at[0], vpair, partner).start()

        return carry

    row = lax.broadcasted_iota(jnp.int32, (128, NB), 0)
    column = lax.broadcasted_iota(jnp.int32, (128, NB), 1)
    factor = jnp.where(
        column < 128,
        jnp.where(column < 64, 0.0, jnp.where(row < 64, -3.0, 0.5)),
        jnp.where(column < 192, 0.0, jnp.where(row < 64, -0.5, 0.0)),
    ) * (1.0 / 1024.0)
    slot = jnp.where(row < 64, row, row - 64)

    def couplings(i, carry):
        e = jnp.where((core == 1) | (i == 3), i, lax.rem(i + 2, 3))
        half = jnp.where(e // 2 == core, 1, 0)
        k = lax.rem(e, 2)

        @pl.when(i == 3)
        def _():
            arrive("lead", 0, tl.at[4])

        order = face_pairing[pl.ds(e, 1), :]
        order = jnp.concatenate([order] * 4, axis=1)
        mixing = jnp.where(slot == order, factor, 0.0).astype(BF16)
        high, low = split(jnp.concatenate([ta[e], tb[e]], axis=1))
        sides = nt(high, mixing) + nt(low, mixing)
        mine = rows(k * NB, NB)
        cpart[half, mine, :] = three(nt, split(sides), split(tl[e + 1]))

        @pl.when(half == 0)
        def _():
            remote("pair", 1 + k, cpart.at[0, mine], cpair.at[mine], partner).start()

        return carry

    sizes = (32, 32, 48)

    def chunk(unit, t, half):
        return rows(lax.rem(unit, 2) * NB + (half * 4 + t) * sizes[unit], sizes[unit])

    def sources(k):
        dx, dy = NEAR[k]
        return lax.rem(x + 4 - dx, 4), yh if dy == 0 else 1 - yh

    def arrived(unit, k):
        return v_in.at[k] if unit == 2 else c_in.at[unit, k]

    def part(unit):
        return vpart.at[1] if unit == 2 else cpart.at[1]

    def block(unit):
        return vblock if unit == 2 else cblock

    def scatter(unit):
        for k in range(7):
            push("scatter", unit * 7 + k, part(unit).at[chunk(unit, *chips[k])], arrived(unit, k), peers[k])

    def reduce(unit):
        where = chunk(unit, x, yh)
        total = part(unit)[where, :]
        for k in (6, 5, 4, 3, 2, 1, 0):
            arrive("scatter", unit * 7 + k, arrived(unit, k))
            total = total + arrived(unit, k)[...]
        block(unit)[where, :] = total

    def gather(unit):
        where = chunk(unit, x, yh)
        for k in range(7):
            push("gather", unit * 7 + k, block(unit).at[where], block(unit).at[where], peers[k])

    def gathered(unit):
        for k in (6, 5, 4, 3, 2, 1, 0):
            arrive("gather", unit * 7 + k, block(unit).at[chunk(unit, *sources(k))])

    def couple(unit):
        where = rows(unit * NB, NB)
        arrive("pair", 1 + unit, cpair.at[where])
        cpart[1, where, :] = cpart[1, where, :] + cpair[where, :]
        scatter(unit)

    def doubled(value):
        high, low = split(value)
        return jnp.concatenate([high, low], axis=1)

    def times(matrix, pair):
        both = nn(matrix[0], pair)
        return both[:, :128] + (both[:, 128:] + nn(matrix[1], pair[:, :128]))

    def halo(name, n, j):
        if name == "up":
            return remote("up", n * 2 + j, up_out.at[n, j], up_in.at[n, j], after)
        return remote("down", n * 2 + j, field.at[n, j, pl.ds(0, 256)], down_in.at[n, j], before)

    def offer_up(n, j):
        up_out[n, j] = times(up_part, doubled(field[n, j, 256:, :]))
        halo("up", n, j).start()

    def meet():
        pl.semaphore_wait(barrier, 11)
        remote("lead", 0, tl.at[0], tl.at[4], em).start()

    depth = lax.rem(elem, 8)
    lax.fori_loop(0, 4, traces, 0)
    pl.when(depth > 0)(meet)
    lax.fori_loop(0, 4, volumes, 0)
    @pl.when(depth == 0)
    def _():
        meet()
        remote("pair", 0, vpart.at[0], vpair, partner).start()

    arrive("pair", 0, vpair)
    vpart[1] = vpart[1] + vpair[...]
    scatter(2)
    own_field.start()
    push("vin", 0, orbitals.at[other_rows], field.at[0, core], partner)
    lax.fori_loop(0, 4, couplings, 0)
    couple(0)
    couple(1)
    reduce(2)
    gather(2)
    reduce(1)
    gather(1)
    reduce(0)
    gather(0)
    gathered(1)
    outer = cblock[NB:, :] * (1.0 / 12.0)
    high, low = split(outer.T)
    up_part[0] = high
    up_part[1] = low
    high, low = split(outer)
    down_part[0] = high
    down_part[1] = low
    own_field.wait()
    arrive("vin", 0, field.at[0, other])
    for j in range(2):
        halo("down", 0, j).start()
        offer_up(0, j)

    diagonal = jnp.where(
        lax.broadcasted_iota(jnp.int32, (128, 128), 0) == lax.broadcasted_iota(jnp.int32, (128, 128), 1), 4.0 / 12.0, 0.0
    )
    def halved(corner):
        return (corner + corner.T) * (0.5 / 12.0) - diagonal

    def near_store(first, second, value):
        high, low = split(value)
        near_part[0, first : first + value.shape[0], second : second + value.shape[1]] = high
        near_part[1, first : first + value.shape[0], second : second + value.shape[1]] = low

    gathered(2)
    for k in range(2):
        first = k * 192
        corner = k * NB
        near_store(corner, corner, halved(vblock[first : first + 128, :128]))
        cross = vblock[first : first + 128, 128:] * (0.5 / 12.0)
        near_store(corner, corner + 128, cross)
        near_store(corner + 128, corner, cross.T)
        last = jnp.concatenate([vblock[first + 128 : first + 192, :128], vblock[first + 128 : first + 192, 128:]], axis=0)
        near_store(corner + 128, corner + 128, halved(last))
    gathered(0)
    inner = cblock[:NB, :] * (1.0 / 12.0)
    near_store(0, NB, inner)
    near_store(NB, 0, inner.T)
    def filter_step(m, carry):
        n = m - 1
        oldest = jnp.maximum(m - 2, 0)
        scale = jnp.where(m == 1, 1.0, 2.0)
        keep = jnp.where(m == 1, 0.0, 1.0)
        parts = [split(field[n, j]) for j in range(2)]
        high = jnp.concatenate([parts[0][0], parts[1][0]], axis=1)
        low = jnp.concatenate([parts[0][1], parts[1][1]], axis=1)
        near_sum[...] = nn(near_part[0], high) + (nn(near_part[0], low) + nn(near_part[1], high))

        def column_step(j, inner):
            lanes = pl.ds(pl.multiple_of(j * 128, 128), 128)
            halo("up", n, j).wait_recv()
            value = scale * (near_sum[:256, lanes] + up_in[n, j])
            field[m, j, :256, :] = value - keep * field[oldest, j, :256, :]

            @pl.when(m < 4)
            def _():
                halo("down", m, j).start()

            halo("down", n, j).wait_recv()
            value = scale * (near_sum[256:, lanes] + times(down_part, doubled(down_in[n, j])))
            field[m, j, 256:, :] = value - keep * field[oldest, j, 256:, :]

            @pl.when(m < 4)
            def _():
                offer_up(m, j)

            @pl.when((m == 4) & (j == other))
            def _():
                remote("vout", 0, field.at[4, other], out.at[own_rows], partner).start()

            return inner

        return lax.fori_loop(0, 2, column_step, carry)

    lax.fori_loop(1, 5, filter_step, 0)
    out[own_rows, :] = field[4, core]

    def drain(k, carry):
        n, j = k // 2, lax.rem(k, 2)
        halo("up", n, j).wait_send()
        halo("down", n, j).wait_send()
        return carry

    lax.fori_loop(0, 8, drain, 0)
    for copy in started:
        copy.wait_send()
    sent("lead", 0, tl.at[0])
    sent("pair", 0, vpart.at[0])
    for unit in range(2):
        sent("pair", 1 + unit, cpart.at[0, rows(unit * NB, NB)])
    sent("vout", 0, field.at[4, other])
    arrive("vout", 0, out.at[other_rows])


def body(basis, applied, quad, face_index, face_pairing, orbitals):
    anywhere = pl.BlockSpec(memory_space=pl.ANY)
    return pl.pallas_call(
        kernel,
        out_shape=pltpu.VMEM(orbitals.shape, F32),
        in_specs=[anywhere] * 6,
        out_specs=pl.BlockSpec(memory_space=pltpu.VMEM),
        scratch_shapes=[
            pltpu.VMEM((4, 512, NB), F32),
            pltpu.VMEM((4, 512, NB), F32),
            pltpu.VMEM(quad.shape, F32),
            pltpu.VMEM(face_index.shape, jnp.int32),
            pltpu.VMEM(face_pairing.shape, jnp.int32),
            pltpu.VMEM((2, 4, NB, 512), BF16),
            pltpu.VMEM((4, NB, 128), F32),
            pltpu.VMEM((4, NB, 128), F32),
            pltpu.VMEM((5, NB, 128), F32),
            pltpu.VMEM((2, 384, NB), F32),
            pltpu.VMEM((2, 512, NB), F32),
            pltpu.VMEM((384, NB), F32),
            pltpu.VMEM((512, NB), F32),
            pltpu.VMEM((7, 48, NB), F32),
            pltpu.VMEM((2, 7, 32, NB), F32),
            pltpu.VMEM((384, NB), F32),
            pltpu.VMEM((512, NB), F32),
            pltpu.VMEM((2, 512, 512), BF16),
            pltpu.VMEM((2, NB, NB), BF16),
            pltpu.VMEM((2, NB, NB), BF16),
            pltpu.VMEM((5, 2, 512, 128), F32),
            pltpu.VMEM((512, NB), F32),
            pltpu.VMEM((4, 2, NB, 128), F32),
            pltpu.VMEM((4, 2, NB, 128), F32),
            pltpu.VMEM((4, 2, NB, 128), F32),
            pltpu.SemaphoreType.DMA((12,)),
            pltpu.SemaphoreType.DMA((COPIES,)),
            pltpu.SemaphoreType.DMA((COPIES,)),
        ],
        name="filtered",
        compiler_params=pltpu.CompilerParams(collective_id=0, has_side_effects=True),
    )(basis, applied, quad, face_index, face_pairing, orbitals)


def solution(mesh):
    return jax.shard_map(
        body,
        mesh=mesh,
        in_specs=(
            P("elem", "pts", None),
            P("elem", "pts", None),
            P("elem", "pts"),
            P("elem", None, "pts"),
            P("elem", "pts"),
            P("elem", "pts"),
        ),
        out_specs=P("elem", "pts"),
        check_vma=False,
    )
```

time: 61.7 us -> 57.4 us (0.930)
  Pallas kernels: 60.8 us -> 56 us
    pallas_call x1, Pallas kernels: 60.8 us -> 56 us  [body(): pl.pallas_call(kernel, out_shape=pltpu.VMEM(orbitals.shape, F32), in_spec...]
where the time goes in v1:
time: 57.4 us; the launch traced here: 56.8 us
  Pallas kernels  56 us (98%)
  local copies, waits for them, and re-layouts  0.8 us (1%)
    pallas_call x1, Pallas kernels, body(): pl.pallas_call(kernel, out_shape=pltpu.VMEM(orbitals.shape, F32), in_spec...  56 us

profile of v1, /device:TPU:1, one launch (start us, length us, event | category | flops | bytes accessed | tf_op | source)
XLA Modules:
  0.0 56.8 jit_solution(7826463852532958406)
XLA Ops:
  0.0 56.0 %filtered.1 = f32[1024,128]{1,0:T(8,128)S(1)} custom-call(f32[4,512,256]{2,1,0:T(8,128)} %basis.1, f32[4,512,256]{2,1,0:T(8,128)} %applied.1, f32[4,512]{1,0:T(4,128)} %quad_in.1, s32[4,4,64]{2,1,0:T(4,128)} %index_in.1, s32[4,64]{1,0:T(4,128)} %pairing_in.1, f32[1024,128]{1,0:T(8,128)} %orbitals.1), custom_call_target="tpu_custom_call" | custom-call | tf_op jit(solution)/shard_map/filtered/pallas_call | solution.py:385
  56.0 0.8 %copy.8 = f32[1024,128]{1,0:T(8,128)} copy(f32[1024,128]{1,0:T(8,128)S(1)} %filtered.1) | data formatting | bytes 1048576

commit v2 on v1

--- a/solution.py
+++ b/solution.py
@@ -8,6 +8,9 @@
 NB = 256
 MESH = pl.DeviceIdType.MESH
 NEAR = ((2, 1), (1, 1), (3, 1), (2, 0), (0, 1), (1, 0), (3, 0))
+ROW = (3, 5, 6)
+COLUMN = 4
+ORDERS = ("direct", "direct", "yx")
 F32 = jnp.float32
 BF16 = jnp.bfloat16
 
@@ -110,6 +113,7 @@
     own_rows = pl.ds(pl.multiple_of(core * 512, 512), 512)
     other_rows = pl.ds(pl.multiple_of(other * 512, 512), 512)
     own_field = pltpu.make_async_copy(orbitals.at[own_rows], field.at[0, core], local.at[8])
+    own_field.start()
 
     barrier = pltpu.get_barrier_semaphore()
     for device in [partner, far, em, ep] + peers:
@@ -118,16 +122,21 @@
     point = lax.broadcasted_iota(jnp.int32, (512, NB), 0)
     lane = lax.broadcasted_iota(jnp.int32, (NB, 128), 1)
 
-    def traces(e, carry):
-        pltpu.make_async_copy(basis.at[e], b_buf.at[e], local.at[e]).wait()
-
-        @pl.when(e == 0)
+    def trace_pair(k, carry):
+        @pl.when(k == 0)
         def _():
             for copy in small:
                 copy.wait()
 
-        later = lax.rem(e + 2 * other, 4)
-        pltpu.make_async_copy(applied.at[later], a_buf.at[later], local.at[4 + later]).start()
+        for e in (2 * k, 2 * k + 1):
+            later = lax.rem(e + 2 * other, 4)
+            pltpu.make_async_copy(basis.at[e], b_buf.at[e], local.at[e]).wait()
+            pltpu.make_async_copy(applied.at[later], a_buf.at[later], local.at[4 + later]).start()
+        traces(2 * k)
+        traces(2 * k + 1)
+        return carry
+
+    def traces(e):
         turned = b_buf[e].T
         high, low = split(turned)
         picks = jnp.concatenate([face_index[e, r : r + 1, :] for r in (0, 2, 1, 3)], axis=1)
@@ -140,16 +149,26 @@
         high, low = split(turned * quad[pl.ds(e, 1), :])
         bq[0, e] = high
         bq[1, e] = low
-        return carry
 
     def rows(first, size):
         return pl.ds(pl.multiple_of(first, 8), size)
 
-    def volumes(i, carry):
-        e = lax.rem(i + 2 * other, 4)
-        half = i // 2
-        first = lax.rem(i, 2) * 192
-        pltpu.make_async_copy(applied.at[e], a_buf.at[e], local.at[4 + e]).wait()
+    def volume_pair(half, carry):
+        for k in range(2):
+            e = lax.rem(2 * half + k + 2 * other, 4)
+            pltpu.make_async_copy(applied.at[e], a_buf.at[e], local.at[4 + e]).wait()
+        volumes(half, 0)
+        volumes(half, 1)
+
+        @pl.when((half == 0) & (depth > 0))
+        def _():
+            remote("pair", 0, vpart.at[0], vpair, partner).start()
+
+        return carry
+
+    def volumes(half, k):
+        e = lax.rem(2 * half + k + 2 * other, 4)
+        first = k * 192
         faces = ta[e]
         total = three(nn, (bq[0, e], bq[1, e]), split(a_buf[e]))
         total = total + three(nt, split((2.0 * faces + tb[e]) * (1.0 / 1024.0)), split(faces))
@@ -157,12 +176,6 @@
         vpart[half, rows(first, 128), 128:] = total[:128, 128:] + total[128:, :128].T
         vpart[half, rows(first + 128, 64), :128] = total[128:192, 128:]
         vpart[half, rows(first + 128, 64), 128:] = total[192:, 128:]
-
-        @pl.when((i == 1) & (depth > 0))
-        def _():
-            remote("pair", 0, vpart.at[0], vpair, partner).start()
-
-        return carry
 
     row = lax.broadcasted_iota(jnp.int32, (128, NB), 0)
     column = lax.broadcasted_iota(jnp.int32, (128, NB), 1)
@@ -226,14 +239,43 @@
             total = total + arrived(unit, k)[...]
         block(unit)[where, :] = total
 
+    def share(unit, slot, where, k):
+        push("gather", unit * 7 + slot, block(unit).at[where], block(unit).at[where], peers[k])
+
     def gather(unit):
         where = chunk(unit, x, yh)
-        for k in range(7):
-            push("gather", unit * 7 + k, block(unit).at[where], block(unit).at[where], peers[k])
+        if ORDERS[unit] == "direct":
+            for k in range(7):
+                share(unit, k, where, k)
+            return
+        for i, k in enumerate(ROW):
+            share(unit, 1 + i, where, k)
+        share(unit, 0, where, COLUMN)
+
+    def forward(unit):
+        if ORDERS[unit] == "yx":
+            where = chunk(unit, x, 1 - yh)
+            arrive("gather", unit * 7, block(unit).at[where])
+            for i, k in enumerate(ROW):
+                share(unit, 4 + i, where, k)
+        if ORDERS[unit] == "xy":
+            for i in (2, 1, 0):
+                where = chunk(unit, sources(ROW[i])[0], yh)
+                arrive("gather", unit * 7 + 1 + i, block(unit).at[where])
+                share(unit, 4 + i, where, COLUMN)
 
     def gathered(unit):
-        for k in (6, 5, 4, 3, 2, 1, 0):
-            arrive("gather", unit * 7 + k, block(unit).at[chunk(unit, *sources(k))])
+        if ORDERS[unit] == "direct":
+            for k in (6, 5, 4, 3, 2, 1, 0):
+                arrive("gather", unit * 7 + k, block(unit).at[chunk(unit, *sources(k))])
+            return
+        for i, k in enumerate(ROW):
+            t, _ = sources(k)
+            if ORDERS[unit] == "yx":
+                arrive("gather", unit * 7 + 1 + i, block(unit).at[chunk(unit, t, yh)])
+            arrive("gather", unit * 7 + 4 + i, block(unit).at[chunk(unit, t, 1 - yh)])
+        if ORDERS[unit] == "xy":
+            arrive("gather", unit * 7, block(unit).at[chunk(unit, x, 1 - yh)])
 
     def couple(unit):
         where = rows(unit * NB, NB)
@@ -261,11 +303,12 @@
     def meet():
         pl.semaphore_wait(barrier, 11)
         remote("lead", 0, tl.at[0], tl.at[4], em).start()
+        remote("vin", 0, orbitals.at[other_rows], field.at[0, core], partner).start()
 
     depth = lax.rem(elem, 8)
-    lax.fori_loop(0, 4, traces, 0)
+    lax.fori_loop(0, 2, trace_pair, 0)
     pl.when(depth > 0)(meet)
-    lax.fori_loop(0, 4, volumes, 0)
+    lax.fori_loop(0, 2, volume_pair, 0)
     @pl.when(depth == 0)
     def _():
         meet()
@@ -274,8 +317,6 @@
     arrive("pair", 0, vpair)
     vpart[1] = vpart[1] + vpair[...]
     scatter(2)
-    own_field.start()
-    push("vin", 0, orbitals.at[other_rows], field.at[0, core], partner)
     lax.fori_loop(0, 4, couplings, 0)
     couple(0)
     couple(1)
@@ -285,6 +326,9 @@
     gather(1)
     reduce(0)
     gather(0)
+    forward(2)
+    forward(1)
+    forward(0)
     gathered(1)
     outer = cblock[NB:, :] * (1.0 / 12.0)
     high, low = split(outer.T)
@@ -373,6 +417,7 @@
     for copy in started:
         copy.wait_send()
     sent("lead", 0, tl.at[0])
+    sent("vin", 0, field.at[0, core])
     sent("pair", 0, vpart.at[0])
     for unit in range(2):
         sent("pair", 1 + unit, cpart.at[0, rows(unit * NB, NB)])

time: 57.4 us -> 56.7 us (0.988)
  no operation moved by 1% of the time
where the time goes in v2:
time: 56.7 us; the launch traced here: 56.6 us
  Pallas kernels  55.8 us (98%)
  local copies, waits for them, and re-layouts  0.8 us (1%)
    pallas_call x1, Pallas kernels, body(): pl.pallas_call(kernel, out_shape=pltpu.VMEM(orbitals.shape, F32), in_spec...  55.8 us

profile of v2, /device:TPU:1, one launch (start us, length us, event | category | flops | bytes accessed | tf_op | source)
XLA Modules:
  0.0 56.6 jit_solution(10480329550882476460)
XLA Ops:
  0.0 55.8 %filtered.1 = f32[1024,128]{1,0:T(8,128)S(1)} custom-call(f32[4,512,256]{2,1,0:T(8,128)} %basis.1, f32[4,512,256]{2,1,0:T(8,128)} %applied.1, f32[4,512]{1,0:T(4,128)} %quad_in.1, s32[4,4,64]{2,1,0:T(4,128)} %index_in.1, s32[4,64]{1,0:T(4,128)} %pairing_in.1, f32[1024,128]{1,0:T(8,128)} %orbitals.1), custom_call_target="tpu_custom_call" | custom-call | tf_op jit(solution)/shard_map/filtered/pallas_call | solution.py:430
  55.8 0.8 %copy.8 = f32[1024,128]{1,0:T(8,128)} copy(f32[1024,128]{1,0:T(8,128)S(1)} %filtered.1) | data formatting | bytes 1048576

commit v3 on v2

--- a/solution.py
+++ b/solution.py
@@ -10,7 +10,7 @@
 NEAR = ((2, 1), (1, 1), (3, 1), (2, 0), (0, 1), (1, 0), (3, 0))
 ROW = (3, 5, 6)
 COLUMN = 4
-ORDERS = ("direct", "direct", "yx")
+ORDERS = ("yx", "direct", "yx")
 F32 = jnp.float32
 BF16 = jnp.bfloat16
 
@@ -47,7 +47,7 @@
     slots = Slots()
     table = {}
     for name, number in (
-        ("lead", 1), ("vin", 1), ("vout", 1), ("pair", 3), ("scatter", 21), ("gather", 21), ("up", 8), ("down", 8),
+        ("lead", 1), ("vin", 1), ("vout", 2), ("pair", 3), ("scatter", 21), ("gather", 21), ("up", 8), ("down", 8),
     ):
         table[name] = slots.take(number)
     return table, slots.count
@@ -368,6 +368,9 @@
     inner = cblock[:NB, :] * (1.0 / 12.0)
     near_store(0, NB, inner)
     near_store(NB, 0, inner.T)
+    def hand_over(k):
+        return remote("vout", k, field.at[4, other, pl.ds(k * NB, NB)], out.at[rows(core * 512 + k * NB, NB)], partner)
+
     def filter_step(m, carry):
         n = m - 1
         oldest = jnp.maximum(m - 2, 0)
@@ -384,6 +387,10 @@
             value = scale * (near_sum[:256, lanes] + up_in[n, j])
             field[m, j, :256, :] = value - keep * field[oldest, j, :256, :]
 
+            @pl.when((m == 4) & (j == other))
+            def _():
+                hand_over(0).start()
+
             @pl.when(m < 4)
             def _():
                 halo("down", m, j).start()
@@ -398,7 +405,7 @@
 
             @pl.when((m == 4) & (j == other))
             def _():
-                remote("vout", 0, field.at[4, other], out.at[own_rows], partner).start()
+                hand_over(1).start()
 
             return inner
 
@@ -421,8 +428,9 @@
     sent("pair", 0, vpart.at[0])
     for unit in range(2):
         sent("pair", 1 + unit, cpart.at[0, rows(unit * NB, NB)])
-    sent("vout", 0, field.at[4, other])
-    arrive("vout", 0, out.at[other_rows])
+    for k in range(2):
+        hand_over(k).wait_send()
+        arrive("vout", k, out.at[rows(other * 512 + k * NB, NB)])
 
 
 def body(basis, applied, quad, face_index, face_pairing, orbitals):

time: 56.7 us -> 56.6 us (level)
  no operation moved by 1% of the time
where the time goes in v3:
time: 56.6 us; the launch traced here: 56.5 us
  Pallas kernels  55.7 us (98%)
  local copies, waits for them, and re-layouts  0.8 us (1%)
    pallas_call x1, Pallas kernels, body(): pl.pallas_call(kernel, out_shape=pltpu.VMEM(orbitals.shape, F32), in_spec...  55.7 us

profile of v3, /device:TPU:1, one launch (start us, length us, event | category | flops | bytes accessed | tf_op | source)
XLA Modules:
  0.0 56.5 jit_solution(9765182793782199421)
XLA Ops:
  0.0 55.7 %filtered.1 = f32[1024,128]{1,0:T(8,128)S(1)} custom-call(f32[4,512,256]{2,1,0:T(8,128)} %basis.1, f32[4,512,256]{2,1,0:T(8,128)} %applied.1, f32[4,512]{1,0:T(4,128)} %quad_in.1, s32[4,4,64]{2,1,0:T(4,128)} %index_in.1, s32[4,64]{1,0:T(4,128)} %pairing_in.1, f32[1024,128]{1,0:T(8,128)} %orbitals.1), custom_call_target="tpu_custom_call" | custom-call | tf_op jit(solution)/shard_map/filtered/pallas_call | solution.py:438
  55.7 0.8 %copy.8 = f32[1024,128]{1,0:T(8,128)} copy(f32[1024,128]{1,0:T(8,128)S(1)} %filtered.1) | data formatting | bytes 1048576

commit v4 on v3

--- a/solution.py
+++ b/solution.py
@@ -328,7 +328,6 @@
     gather(0)
     forward(2)
     forward(1)
-    forward(0)
     gathered(1)
     outer = cblock[NB:, :] * (1.0 / 12.0)
     high, low = split(outer.T)
@@ -342,6 +341,7 @@
     for j in range(2):
         halo("down", 0, j).start()
         offer_up(0, j)
+    forward(0)
 
     diagonal = jnp.where(
         lax.broadcasted_iota(jnp.int32, (128, 128), 0) == lax.broadcasted_iota(jnp.int32, (128, 128), 1), 4.0 / 12.0, 0.0

time: 56.6 us -> 56.4 us (level)
  no operation moved by 1% of the time
where the time goes in v4:
time: 56.4 us; the launch traced here: 56.3 us
  Pallas kernels  55.5 us (98%)
  local copies, waits for them, and re-layouts  0.8 us (1%)
    pallas_call x1, Pallas kernels, body(): pl.pallas_call(kernel, out_shape=pltpu.VMEM(orbitals.shape, F32), in_spec...  55.5 us

profile of v4, /device:TPU:1, one launch (start us, length us, event | category | flops | bytes accessed | tf_op | source)
XLA Modules:
  0.0 56.3 jit_solution(7370096162143423224)
XLA Ops:
  0.0 55.5 %filtered.1 = f32[1024,128]{1,0:T(8,128)S(1)} custom-call(f32[4,512,256]{2,1,0:T(8,128)} %basis.1, f32[4,512,256]{2,1,0:T(8,128)} %applied.1, f32[4,512]{1,0:T(4,128)} %quad_in.1, s32[4,4,64]{2,1,0:T(4,128)} %index_in.1, s32[4,64]{1,0:T(4,128)} %pairing_in.1, f32[1024,128]{1,0:T(8,128)} %orbitals.1), custom_call_target="tpu_custom_call" | custom-call | tf_op jit(solution)/shard_map/filtered/pallas_call | solution.py:438
  55.5 0.8 %copy.8 = f32[1024,128]{1,0:T(8,128)} copy(f32[1024,128]{1,0:T(8,128)S(1)} %filtered.1) | data formatting | bytes 1048576
